TPU v7x, 256 devices: a whole 4x4x8 slice. The times are simulated.
256 devices in a mesh: modes: 32 (over z_lo, y, core), dom: 8 (over x, z_hi).
Axes of the slice: x: 4, y: 4, z: 8 (z_hi: 2, z_lo: 4; z = z_hi * 4 + z_lo), core: 2. Of those that a mesh axis runs over, the one named last changes fastest.
Arguments:
- velocity: float32 [3, 512, 81, 1024], P(None, 'modes', None, 'dom'), may hold values from -6 to 6
- slot_of_cell: int32 [8, 128], P('dom'), may hold values from 0 to 127, each once within a row
- elem_mats: float32 [4, 81, 81], replicated, may hold values from -0.625 to 0.625
- geometry: float32 [4, 1024], P(None, 'dom'), may hold values from 0.5 to 2
Outputs:
- result: float32 [3, 512, 81, 1024], P(None, 'modes', None, 'dom')
Inputs may be any that keep to these rules, and one draw needn't show every extreme that they name: `slot_of_cell`: each row is a permutation of the slots 0 to 127.
All inputs are finite; a program needn't handle non-finite values.
Results may differ from a plain program's by a relative error of at most 0.0003.
Values sent between devices are 32-bit elements; how exact they have to be, the bound alone decides.
A program may use at most 128 MiB of HBM per device.

v0:
```python
import functools

import jax
import jax.numpy as jnp
import numpy as np
from jax import lax
from jax.experimental import pallas as pl
from jax.experimental.pallas import tpu as pltpu
from jax.sharding import PartitionSpec as P

MESH = pl.DeviceIdType.MESH
F32, BF16 = jnp.float32, jnp.bfloat16
LANES = 128
EY = 8
ROWS = 64
NODES = 81
TALL = 88


def coupling(length):
    index = np.arange(length)
    half = length // 2
    wave = np.where(index <= half, index, index - half)
    angle = 2.0 * np.pi * ((wave[:, None] * index[None, :]) % length) / length
    table = np.where((index <= half)[:, None], np.cos(angle), np.sin(angle))
    weight = np.where((index == 0) | (index == half), 1.0, 2.0) / length
    scale = weight * (8.0 * wave / length) ** 2
    return (table.T * scale) @ table


def halves(x):
    high = x.astype(BF16)
    return high, (x - high.astype(F32)).astype(BF16)


def turn(value, shift):
    shift = shift % LANES
    return pltpu.roll(value, shift, 1) if shift else value


def homes(count):
    return [8, 19, 13, 22, 3, 28] if count == 32 else list(range(6))


def kernel(
    count, doms, depth,
    slot_ref, geo_ref, mats_ref, chi_hbm, clo_hbm, vel_hbm, out_hbm,
    vel, chi, clo, stage, lhs, rhs, tall,
    w, we, v, ve, x, xe, back, backe, q, qe, to_left, to_right, from_left, from_right, out,
    load, send1, recv1, send2, recv2, send_e, recv_e, send_f, recv_f, store,
):
    half = ROWS // 2 // count
    length = depth * count
    me, dom = lax.axis_index("modes"), lax.axis_index("dom")
    after, before = lax.rem(dom + 1, doms), lax.rem(dom + doms - 1, doms)
    home = homes(count)
    far = [2, 1, 3, 0] if count == 32 else list(range(count // 8))

    def remote(src, dst, send, recv, modes, where):
        return pltpu.make_async_remote_copy(
            src_ref=src, dst_ref=dst, send_sem=send, recv_sem=recv, device_id=(modes, where), device_id_type=MESH
        )

    def drain(sem, ref):
        pltpu.make_async_copy(ref, ref, sem).wait()

    def peers(act):
        def some(low, _):
            for high in far:
                z = lax.rem(me // 8 + high, len(far))
                d = z * 8 + lax.rem(lax.rem(me, 8) + low, 8)
                if high:
                    act(d)
                else:
                    pl.when(low > 0)(lambda: act(d))
            return 0

        lax.fori_loop(0, 8, some, 0)

    loads = [pltpu.make_async_copy(vel_hbm.at[c], vel.at[c], load.at[c]) for c in range(3)]
    loads += [pltpu.make_async_copy(chi_hbm, chi, load.at[3]), pltpu.make_async_copy(clo_hbm, clo, load.at[4])]
    for copy in loads:
        copy.start()
    barrier = pltpu.get_barrier_semaphore()
    for other in (before, after):
        pl.semaphore_signal(barrier, inc=1, device_id=(me, other), device_id_type=MESH)
    peers(lambda d: pl.semaphore_signal(barrier, inc=1, device_id=(d, dom), device_id_type=MESH))

    wide = lax.broadcasted_iota(jnp.int32, (TALL, LANES), 1)

    def stack(t):
        stage[...] = jnp.zeros_like(stage)
        for i in range(8):
            stage[8 * i : 8 * i + 8, 0:NODES] = mats_ref[t, 9 * i : 9 * i + 8, :]
            stage[72 + i : 73 + i, 0:NODES] = mats_ref[t, 9 * i + 8 : 9 * i + 9, :]
        stage[64:72, 0:NODES] = mats_ref[t, 72:80, :]
        stage[80:81, 0:NODES] = mats_ref[t, 80:81, :]
        full = stage[...]
        high = full.astype(BF16).astype(F32)
        low = full - high
        low_turned = turn(low, 80)
        first = jnp.where(wide < 80, high, low_turned)
        second = jnp.where(wide < 32, low_turned, turn(high, 32))
        second = jnp.where(wide == 113, turn(low, 33), jnp.where(wide == 114, turn(high, 34), second))
        second = jnp.where(wide < 115, second, 0.0)
        lhs[TALL * t : TALL * t + TALL, 0:LANES] = first.astype(BF16)
        lhs[TALL * t : TALL * t + TALL, LANES:] = second.astype(BF16)

    stack(3)
    slots = jnp.broadcast_to(slot_ref[0:1, :], (80, LANES))
    geo = [
        jnp.take_along_axis(jnp.broadcast_to(geo_ref[t : t + 1, :], (8, LANES)), slots[0:8], axis=1)[0:1] for t in range(4)
    ]
    row16 = lax.broadcasted_iota(jnp.int32, (16, LANES), 0)
    lane = lax.broadcasted_iota(jnp.int32, (depth, LANES), 1)
    inner, upper = lane >= EY, lane % EY >= 1

    def columns(c, p):
        def product(lo, size):
            part = lambda m: vel[m, pl.ds(lo * depth + p, size, stride=depth), :]
            return jnp.take_along_axis(part(c) * part(lax.rem(c + 1, 3)), slots[0:size], axis=1)

        high, low = halves(product(0, 80))
        last = product(73, 8)[7:8]
        last_high = last.astype(BF16).astype(F32)
        rest = jnp.where(row16 < 2, last_high, jnp.where(row16 == 2, last - last_high, 0.0))
        return jnp.concatenate([high, high, low, rest.astype(BF16)], axis=0)

    def assemble(rows, ends):
        at = lambda r: tall[r * depth : r * depth + depth, :]
        corner = at(80)
        edge = jnp.zeros((depth, LANES), F32)
        face = jnp.where(lane == 64, turn(corner, 65), 0.0)
        for i in range(8):
            top = at(72 + i)
            if i == 0:
                top = top + jnp.where(inner, turn(corner, EY), 0.0)
            edge = jnp.where(lane % EY == i, turn(top, i - 7), edge)
            for j in range(8):
                value = at(8 * i + j)
                if i == 0:
                    value = value + jnp.where(inner, turn(at(64 + j), EY), 0.0)
                if j == 0:
                    value = value + jnp.where(upper, turn(top, 1), 0.0)
                rows(8 * i + j, value)
        for j in range(8):
            right = at(64 + j)
            if j == 0:
                right = right + jnp.where(upper, turn(corner, 1), 0.0)
            face = jnp.where(lane // EY == j, turn(right, EY + EY * j), face)
        ends(edge, face)

    def mass(c):
        scale = jnp.broadcast_to(geo[3], (TALL, LANES))

        def pair(step, _):
            block = jnp.concatenate([columns(c, 2 * step), columns(c, 2 * step + 1)], axis=1)
            rhs[c * (depth // 2) + step] = block
            image = jnp.dot(lhs[3 * TALL :, :], block, preferred_element_type=F32)
            for h in range(2):
                tall[pl.ds(2 * step + h, TALL, stride=depth), :] = image[:, LANES * h : LANES * h + LANES] * scale
            return 0

        lax.fori_loop(0, depth // 2, pair, 0, unroll=2)

        def rows(r, value):
            w[c, r // (half * count) , r % (half * count) // half, r % half] = value

        def ends(edge, face):
            we[2 * c], we[2 * c + 1] = edge, face

        assemble(rows, ends)

    def stiff(c):
        scale = [jnp.broadcast_to(g, (TALL, LANES)) for g in geo]

        def pair(step, _):
            image = jnp.dot(lhs[...], rhs[c * (depth // 2) + step], preferred_element_type=F32)
            for h in range(2):
                part = image[:, LANES * h : LANES * h + LANES]
                terms = [part[TALL * t : TALL * t + TALL] * scale[t] for t in range(4)]
                tall[pl.ds(2 * step + h, TALL, stride=depth), :] = (terms[0] + terms[1]) + (terms[2] + terms[3])
            return 0

        lax.fori_loop(0, depth // 2, pair, 0, unroll=2)

        def rows(r, value):
            v[c, r] = value

        def ends(edge, face):
            ve[2 * c], ve[2 * c + 1] = edge, face

        assemble(rows, ends)

    def send_both(c):
        peers(lambda d: remote(w.at[c, :, d], x.at[c, :, me], send1.at[c], recv1.at[c], d, dom).start())

    def send_half(h):
        peers(lambda d: remote(w.at[2, h, d], x.at[2, h, me], send1.at[2 + h], recv1.at[2 + h], d, dom).start())

    def send_ends(c):
        for k in range(2):
            for n in range(3):
                @pl.when((c == n) & (me != home[2 * n + k]))
                def _():
                    e = 2 * n + k
                    remote(we.at[e], xe.at[me], send_e.at[e], recv_e.at[6], home[e], dom).start()

    loads[0].wait()
    loads[1].wait()
    mass(0)
    pl.semaphore_wait(barrier, count + 1)
    send_both(0)
    send_ends(0)
    loads[2].wait()

    def others(c, _):
        mass(c)

        @pl.when(c == 1)
        def _():
            send_both(1)

        send_ends(c)
        return 0

    lax.fori_loop(1, 3, others, 0)
    send_half(0)
    send_half(1)
    for t in range(3):
        stack(t)

    def stiffs(c, _):
        stiff(c)
        return 0

    lax.fori_loop(0, 3, stiffs, 0)

    loads[3].wait()
    loads[4].wait()

    def apply(value):
        high, low = halves(value)
        dot = functools.partial(jnp.dot, preferred_element_type=F32)
        return dot(chi[...], high) + (dot(clo[...], high) + dot(chi[...], low))

    for c in range(2):
        for h in range(2):
            x[c, h, me] = w[c, h, me]
    for h in range(2):
        x[2, h, me] = w[2, h, me]

    def transform(c, h):
        places = [(0, r) for r in range(half)] + [(1, r) for r in range(half)] if h is None else [(h, r) for r in range(half)]
        for n in range(0, len(places), 2):
            two = places[n : n + 2]
            value = apply(jnp.concatenate([x[c, a, :, r].reshape(length, LANES) for a, r in two], axis=1))
            for k, (a, r) in enumerate(two):
                back[c, a, :, r] = value[:, LANES * k : LANES * k + LANES].reshape(count, depth, LANES)

    for c in range(2):
        drain(recv1.at[c], x.at[c, :, pl.ds(0, count - 1)])
        transform(c, None)
        peers(lambda s: remote(back.at[c, :, s], q.at[c, :, me], send2.at[c], recv2.at[c], s, dom).start())

    for e in range(6):
        @pl.when(me == home[e])
        def _():
            xe[me] = we[e]
            drain(recv_e.at[6], xe.at[pl.ds(0, count - 1)])
            backe[...] = apply(xe[...].reshape(length, LANES)).reshape(count, depth, LANES)
            qe[e] = backe[me]
            peers(lambda s: remote(backe.at[s], qe.at[e], send_e.at[6], recv_e.at[e], s, dom).start())

    for h in range(2):
        drain(recv1.at[2 + h], x.at[2, h, pl.ds(0, count - 1)])
        transform(2, h)
        peers(lambda s: remote(back.at[2, h, s], q.at[2, h, me], send2.at[2 + h], recv2.at[2 + h], s, dom).start())
    for c in range(3):
        for h in range(2):
            q[c, h, me] = back[c, h, me]

    square = lax.broadcasted_iota(jnp.int32, (LANES, LANES), 0)
    hot = (jnp.broadcast_to(slot_ref[0:1, :], (LANES, LANES)) == square).astype(BF16)
    index = lane.astype(F32).astype(BF16)
    inverse = lax.dot_general(index, hot, (((1,), (1,)), ((), ())), preferred_element_type=F32).astype(jnp.int32)
    below, lower = lane < LANES - EY, lane % EY < 7

    def row(c, r):
        return v[c, r] + q[c, r // (half * count), r % (half * count) // half, r % half]

    def faces(c):
        return [
            remote(to_left.at[c], from_right.at[c], send_f.at[2 * c], recv_f.at[2 * c], me, before),
            remote(to_right.at[c], from_left.at[c], send_f.at[2 * c + 1], recv_f.at[2 * c + 1], me, after),
        ]

    def send_faces(c):
        for k in range(2):
            e = 2 * c + k
            pl.when(me != home[e])(lambda: drain(recv_e.at[e], qe.at[0]))
            ve[e] = ve[e] + qe[e]
        value = turn(ve[2 * c], 64)
        for j in range(8):
            value = jnp.where(lane // EY == j, turn(row(c, j), EY * j), value)
        to_left[c] = value
        to_right[c] = ve[2 * c + 1]
        for copy in faces(c):
            copy.start()

    def expand(c, low, high):
        def put(n, value):
            out[c, n] = jnp.take_along_axis(value, inverse, axis=1)

        came = from_left[c]
        edge = ve[2 * c] + jnp.where(lane == 0, turn(came, 64), 0.0)
        if low == 0:
            face = ve[2 * c + 1] + from_right[c]
        for i in range(low, high):
            for j in range(8):
                value = row(c, 8 * i + j)
                if i == 0:
                    value = value + jnp.where(lane < EY, turn(came, -EY * j), 0.0)
                    right = jnp.where(below, turn(value, -EY), turn(face, LANES - EY - EY * j))
                    put(72 + j, right)
                if j == 0:
                    top = jnp.where(lower, turn(value, -1), turn(edge, 7 - i))
                    put(9 * i + 8, top)
                    if i == 0:
                        corner = jnp.where(below, turn(top, -EY), turn(face, 63))
                        put(80, jnp.where(lower, turn(right, -1), corner))
                put(9 * i + j, value)

    stores = [pltpu.make_async_copy(out.at[c], out_hbm.at[c], store.at[c]) for c in range(2)]
    stores.append(pltpu.make_async_copy(out.at[2, 0:36], out_hbm.at[2, 0:36], store.at[2]))
    stores.append(pltpu.make_async_copy(out.at[2, 72:], out_hbm.at[2, 72:], store.at[3]))
    stores.append(pltpu.make_async_copy(out.at[2, 36:72], out_hbm.at[2, 36:72], store.at[4]))
    rest = pl.ds(0, count - 1)
    for c in range(2):
        drain(recv2.at[c], q.at[c, :, rest])
        send_faces(c)
    for c in range(2):
        for copy in faces(c):
            copy.wait()
        expand(c, 0, 8)
        stores[c].start()
    drain(recv2.at[2], q.at[2, 0, rest])
    send_faces(2)
    for copy in faces(2):
        copy.wait()
    expand(2, 0, 4)
    stores[2].start()
    stores[3].start()
    drain(recv2.at[3], q.at[2, 1, rest])
    expand(2, 4, 8)
    stores[4].start()

    for c in range(2):
        drain(send1.at[c], x.at[c, :, rest])
        drain(send2.at[c], x.at[c, :, rest])
        drain(send1.at[2 + c], x.at[2, 0, rest])
        drain(send2.at[2 + c], x.at[2, 0, rest])
    for e in range(6):
        pl.when(me != home[e])(lambda: drain(send_e.at[e], we.at[0]))
        pl.when(me == home[e])(lambda: drain(send_e.at[6], xe.at[rest]))
    for copy in stores:
        copy.wait()


def step(slots, geometry, mats, chi, clo, velocity):
    count, doms = lax.axis_size("modes"), lax.axis_size("dom")
    depth = velocity.shape[1] // NODES
    half = ROWS // 2 // count
    wire = (3, 2, count, half, depth, LANES)
    ends = (6, depth, LANES)
    single = (count, depth, LANES)
    face = (3, depth, LANES)
    vmem, dma = pltpu.VMEM, pltpu.SemaphoreType.DMA
    here, there = pl.BlockSpec(memory_space=pltpu.VMEM), pl.BlockSpec(memory_space=pl.ANY)
    return pl.pallas_call(
        functools.partial(kernel, count, doms, depth),
        in_specs=[here] * 3 + [there] * 3,
        out_specs=there,
        out_shape=jax.ShapeDtypeStruct((3, NODES, depth, LANES), F32),
        scratch_shapes=[
            vmem((3, NODES * depth, LANES), F32),
            vmem(chi.shape, BF16),
            vmem(clo.shape, BF16),
            vmem((TALL, LANES), F32),
            vmem((4 * TALL, 2 * LANES), BF16),
            vmem((3 * depth // 2, 256, 2 * LANES), BF16),
            vmem((TALL * depth, LANES), F32),
            vmem(wire, F32),
            vmem(ends, F32),
            vmem((3, ROWS, depth, LANES), F32),
            vmem(ends, F32),
            vmem(wire, F32),
            vmem(single, F32),
            vmem(wire, F32),
            vmem(single, F32),
            vmem(wire, F32),
            vmem(ends, F32),
            vmem(face, F32),
            vmem(face, F32),
            vmem(face, F32),
            vmem(face, F32),
            vmem((3, NODES, depth, LANES), F32),
            dma((5,)),
            dma((4,)),
            dma((4,)),
            dma((4,)),
            dma((4,)),
            dma((7,)),
            dma((7,)),
            dma((6,)),
            dma((6,)),
            dma((5,)),
        ],
        compiler_params=pltpu.CompilerParams(collective_id=0, has_side_effects=True),
        name="step",
    )(slots, geometry, mats, chi, clo, velocity)


def body(velocity, slot_of_cell, elem_mats, geometry):
    depth = velocity.shape[1]
    table = coupling(depth * lax.axis_size("modes"))
    chi = np.asarray(table, np.float32).astype(jnp.bfloat16)
    clo = (table - chi.astype(np.float64)).astype(np.float32).astype(jnp.bfloat16)
    flat = jnp.swapaxes(velocity, 1, 2).reshape(3, NODES * depth, LANES)
    result = step(slot_of_cell, geometry, elem_mats, jnp.asarray(chi), jnp.asarray(clo), flat)
    return jnp.swapaxes(result, 1, 2)


def solution(mesh):
    in_specs = (P(None, "modes", None, "dom"), P("dom", None), P(), P(None, "dom"))
    out_specs = P(None, "modes", None, "dom")
    return jax.shard_map(body, mesh=mesh, in_specs=in_specs, out_specs=out_specs, check_vma=False)
```

profile of v0, /device:TPU:1, one launch (start us, length us, event | category | flops | bytes accessed | tf_op | source)
XLA Modules:
  0.0 98.0 jit_solution(18034016400212105522)
XLA Ops:
  0.0 1.6 %copy.7.mats_ref = f32[4,81,81]{2,1,0:T(8,128)} copy(f32[4,81,81]{2,0,1:T(4,128)} %param.8) | data formatting | bytes 209952 | tf_op args[2]
  1.6 93.4 %step.1 = f32[3,81,16,128]{3,2,1,0:T(8,128)} custom-call(s32[1,128]{1,0:T(1,128)} %slot_ref.1, f32[4,128]{1,0:T(4,128)} %geo_ref.1, f32[4,81,81]{2,1,0:T(8,128)} %copy.7.mats_ref, bf16[512,512]{1,0:T(8,128)(2,1)} %constant.4.clone.chi_hbm, bf16[512,512]{1,0:T(8,128)(2,1)} %constant.5.clone.clo_hbm, f32[3,1296,128]{2,1,0:T(8,128)} %bitcast.5), custom_call_target="tpu_custom_call" | custom-call | tf_op jit(solution)/shard_map/step/pallas_call | solution.py:380
  95.0 3.0 %copy.9 = f32[3,16,81,128]{3,1,2,0:T(8,128)} copy(f32[3,16,81,128]{3,1,2,0:T(8,128)} %bitcast.4) | data formatting | bytes 3981312
where the time goes:
time: 98.3 us; the launch traced here: 98 us
  Pallas kernels  93.4 us (95%)
  local copies, waits for them, and re-layouts  4.6 us (5%)
    pallas_call x1, Pallas kernels, step(): pl.pallas_call(functools.partial(kernel, count, doms, depth), in_specs=[h...  93.4 us
    unnamed x2, local copies, waits for them, and re-layouts  4.6 us

commit v1 on v0

v1 whole, which is shorter than its diff:
```python
import functools

import jax
import jax.numpy as jnp
import numpy as np
from jax import lax
from jax.experimental import pallas as pl
from jax.experimental.pallas import tpu as pltpu
from jax.sharding import PartitionSpec as P

MESH = pl.DeviceIdType.MESH
F32, BF16 = jnp.float32, jnp.bfloat16
LANES = 128
EY = 8
ROWS = 64
NODES = 81
TALL = 88


def coupling(length):
    index = np.arange(length)
    half = length // 2
    wave = np.where(index <= half, index, index - half)
    angle = 2.0 * np.pi * ((wave[:, None] * index[None, :]) % length) / length
    table = np.where((index <= half)[:, None], np.cos(angle), np.sin(angle))
    weight = np.where((index == 0) | (index == half), 1.0, 2.0) / length
    scale = weight * (8.0 * wave / length) ** 2
    return (table.T * scale) @ table


def halves(x):
    high = x.astype(BF16)
    return high, (x - high.astype(F32)).astype(BF16)


def turn(value, shift):
    shift = shift % LANES
    return pltpu.roll(value, shift, 1) if shift else value


def homes(count):
    return [8, 19, 13, 22, 3, 28] if count == 32 else list(range(6))


def place(c, i, j):
    if i == 0:
        return 8 * c + j
    if c == 0:
        return 24 + 8 * i + j
    if c == 1:
        return 80 + 8 * i + j
    return (30 + j if j < 2 else 190 + j) if i == 7 else 136 + 8 * i + j


def kernel(
    count, doms, depth,
    slot_hbm, geo_hbm, mats_hbm, chi_hbm, clo_hbm, vel_hbm, out_hbm,
    slot_ref, geo_ref, mats_ref, vel, chi, clo, stage, lhs, rhs, tall,
    w, we, v, ve, x, xe, back, backe, q, qe, to_left, to_right, from_left, from_right, out,
    load, send1, recv1, send2, recv2, send_e, recv_e, send_f, recv_f, store,
):
    unit = 32 // count
    chunks = [(0, 1), (1, 2), (2, 3), (3, 5), (5, 6)]
    spans = [(unit * a, unit * (b - a)) for a, b in chunks]
    length = depth * count
    me, dom = lax.axis_index("modes"), lax.axis_index("dom")
    after, before = lax.rem(dom + 1, doms), lax.rem(dom + doms - 1, doms)
    home = homes(count)
    far = [2, 1, 3, 0] if count == 32 else list(range(count // 8))

    def remote(src, dst, send, recv, modes, where):
        return pltpu.make_async_remote_copy(
            src_ref=src, dst_ref=dst, send_sem=send, recv_sem=recv, device_id=(modes, where), device_id_type=MESH
        )

    def drain(sem, ref):
        pltpu.make_async_copy(ref, ref, sem).wait()

    def peers(act):
        def some(low, _):
            for high in far:
                z = lax.rem(me // 8 + high, len(far))
                d = z * 8 + lax.rem(lax.rem(me, 8) + low, 8)
                if high:
                    act(d)
                else:
                    pl.when(low > 0)(lambda: act(d))
            return 0

        lax.fori_loop(0, 8, some, 0)

    loads = [pltpu.make_async_copy(vel_hbm.at[c], vel.at[c], load.at[c]) for c in range(3)]
    loads += [pltpu.make_async_copy(chi_hbm, chi, load.at[3]), pltpu.make_async_copy(clo_hbm, clo, load.at[4])]
    small = ((slot_hbm, slot_ref), (geo_hbm, geo_ref), (mats_hbm, mats_ref))
    loads += [pltpu.make_async_copy(src, dst, load.at[5 + n]) for n, (src, dst) in enumerate(small)]
    barrier = pltpu.get_barrier_semaphore()
    for other in (before, after):
        pl.semaphore_signal(barrier, inc=1, device_id=(me, other), device_id_type=MESH)
    peers(lambda d: pl.semaphore_signal(barrier, inc=1, device_id=(d, dom), device_id_type=MESH))
    for n in (7, 5, 6, 0, 1, 2, 3, 4):
        loads[n].start()
    for n in (5, 6, 7):
        loads[n].wait()

    wide = lax.broadcasted_iota(jnp.int32, (TALL, LANES), 1)

    def stack(t):
        stage[...] = jnp.zeros_like(stage)
        for i in range(8):
            stage[8 * i : 8 * i + 8, 0:NODES] = mats_ref[9 * i : 9 * i + 8, t, :]
            stage[72 + i : 73 + i, 0:NODES] = mats_ref[9 * i + 8 : 9 * i + 9, t, :]
        stage[64:72, 0:NODES] = mats_ref[72:80, t, :]
        stage[80:81, 0:NODES] = mats_ref[80:81, t, :]
        full = stage[...]
        high = full.astype(BF16).astype(F32)
        low = full - high
        low_turned = turn(low, 80)
        first = jnp.where(wide < 80, high, low_turned)
        second = jnp.where(wide < 32, low_turned, turn(high, 32))
        second = jnp.where(wide == 113, turn(low, 33), jnp.where(wide == 114, turn(high, 34), second))
        second = jnp.where(wide < 115, second, 0.0)
        lhs[TALL * t : TALL * t + TALL, 0:LANES] = first.astype(BF16)
        lhs[TALL * t : TALL * t + TALL, LANES:] = second.astype(BF16)

    stack(3)
    slots = jnp.broadcast_to(slot_ref[0:1, :], (80, LANES))
    geo = [
        jnp.take_along_axis(jnp.broadcast_to(geo_ref[t : t + 1, :], (8, LANES)), slots[0:8], axis=1)[0:1] for t in range(4)
    ]
    row16 = lax.broadcasted_iota(jnp.int32, (16, LANES), 0)
    lane = lax.broadcasted_iota(jnp.int32, (depth, LANES), 1)
    inner, upper = lane >= EY, lane % EY >= 1

    def columns(c, p):
        def product(lo, size):
            part = lambda m: vel[m, pl.ds(lo * depth + p, size, stride=depth), :]
            return jnp.take_along_axis(part(c) * part((c + 1) % 3), slots[0:size], axis=1)

        high, low = halves(product(0, 80))
        last = product(73, 8)[7:8]
        last_high = last.astype(BF16).astype(F32)
        rest = jnp.where(row16 < 2, last_high, jnp.where(row16 == 2, last - last_high, 0.0))
        return jnp.concatenate([high, high, low, rest.astype(BF16)], axis=0)

    def assemble(rows, ends):
        at = lambda r: tall[r * depth : r * depth + depth, :]
        corner = at(80)
        edge = jnp.zeros((depth, LANES), F32)
        face = jnp.where(lane == 64, turn(corner, 65), 0.0)
        for i in range(8):
            top = at(72 + i)
            if i == 0:
                top = top + jnp.where(inner, turn(corner, EY), 0.0)
            edge = jnp.where(lane % EY == i, turn(top, i - 7), edge)
            for j in range(8):
                value = at(8 * i + j)
                if i == 0:
                    value = value + jnp.where(inner, turn(at(64 + j), EY), 0.0)
                if j == 0:
                    value = value + jnp.where(upper, turn(top, 1), 0.0)
                rows(i, j, value)
        for j in range(8):
            right = at(64 + j)
            if j == 0:
                right = right + jnp.where(upper, turn(corner, 1), 0.0)
            face = jnp.where(lane // EY == j, turn(right, EY + EY * j), face)
        ends(edge, face)

    def mass(c):
        scale = jnp.broadcast_to(geo[3], (TALL, LANES))

        def pair(step, _):
            block = jnp.concatenate([columns(c, 2 * step), columns(c, 2 * step + 1)], axis=1)
            rhs[c * (depth // 2) + step] = block
            image = jnp.dot(lhs[3 * TALL :, :], block, preferred_element_type=F32)
            for h in range(2):
                tall[pl.ds(2 * step + h, TALL, stride=depth), :] = image[:, LANES * h : LANES * h + LANES] * scale
            return 0

        lax.fori_loop(0, depth // 2, pair, 0, unroll=2)

        def rows(i, j, value):
            n = place(c, i, j)
            if n < 192:
                w[n // count, n % count] = value
            else:
                we[n - 192] = value

        def ends(edge, face):
            for k, value in enumerate((edge, face)):
                w[(24 + 2 * c + k) // count, (24 + 2 * c + k) % count] = value

        assemble(rows, ends)

    def stiff(c):
        scale = [jnp.broadcast_to(g, (TALL, LANES)) for g in geo]

        def pair(step, _):
            image = jnp.dot(lhs[...], rhs[c * (depth // 2) + step], preferred_element_type=F32)
            for h in range(2):
                part = image[:, LANES * h : LANES * h + LANES]
                terms = [part[TALL * t : TALL * t + TALL] * scale[t] for t in range(4)]
                tall[pl.ds(2 * step + h, TALL, stride=depth), :] = (terms[0] + terms[1]) + (terms[2] + terms[3])
            return 0

        lax.fori_loop(0, depth // 2, pair, 0, unroll=2)

        def rows(i, j, value):
            v[c, 8 * i + j] = value

        def ends(edge, face):
            ve[2 * c], ve[2 * c + 1] = edge, face

        assemble(rows, ends)

    def go(n):
        a, size = spans[n]
        peers(lambda d: remote(w.at[pl.ds(a, size), d], x.at[pl.ds(a, size), me], send1.at[n], recv1.at[n], d, dom).start())

    def come(n):
        a, size = spans[n]
        peers(lambda s: remote(back.at[pl.ds(a, size), s], q.at[pl.ds(a, size), me], send2.at[n], recv2.at[n], s, dom).start())

    rest = pl.ds(0, count - 1)

    def arrived(sem, ref, n):
        drain(sem.at[n], ref.at[pl.ds(*spans[n]), rest])

    loads[0].wait()
    loads[1].wait()
    mass(0)
    pl.semaphore_wait(barrier, count + 1)
    go(1)
    loads[2].wait()
    mass(1)
    mass(2)
    go(0)
    for e in range(6):
        @pl.when(me != home[e])
        def _():
            remote(we.at[e], xe.at[me], send_e.at[e], recv_e.at[6], home[e], dom).start()
    go(2)
    for t in range(3):
        stack(t)
    for c in range(3):
        stiff(c)
    loads[3].wait()
    loads[4].wait()

    def apply(value):
        high, low = halves(value)
        dot = functools.partial(jnp.dot, preferred_element_type=F32)
        return dot(chi[...], high) + (dot(clo[...], high) + dot(chi[...], low))

    def transform(n):
        a, size = spans[n]
        arrived(recv1, x, n)
        for r in range(a, a + size):
            x[r, me] = w[r, me]
        for r in range(a, a + size, 2):
            two = range(r, min(r + 2, a + size))
            value = apply(jnp.concatenate([x[k].reshape(length, LANES) for k in two], axis=1))
            for m, k in enumerate(two):
                back[k] = value[:, LANES * m : LANES * m + LANES].reshape(count, depth, LANES)
        for r in range(a, a + size):
            q[r, me] = back[r, me]

    square = lax.broadcasted_iota(jnp.int32, (LANES, LANES), 0)
    hot = (jnp.broadcast_to(slot_ref[0:1, :], (LANES, LANES)) == square).astype(BF16)
    index = lane.astype(F32).astype(BF16)
    inverse = lax.dot_general(index, hot, (((1,), (1,)), ((), ())), preferred_element_type=F32).astype(jnp.int32)
    below, lower = lane < LANES - EY, lane % EY < 7
    lane8 = lane[0:8]

    def row(c, i, j):
        n = place(c, i, j)
        return v[c, 8 * i + j] + (q[n // count, n % count] if n < 192 else qe[n - 192])

    faces = [
        remote(to_left, from_right, send_f.at[0], recv_f.at[0], me, before),
        remote(to_right, from_left, send_f.at[1], recv_f.at[1], me, after),
    ]

    def pack(ref, values):
        last = jnp.zeros((8, LANES), F32)
        for c, value in enumerate(values):
            upper_planes, lower_planes = value[0:8], value[8:16]
            ref[c] = jnp.where(lane8 < 64, upper_planes, turn(lower_planes, 64))
            last = jnp.where(lane8 == 2 * c, turn(upper_planes, 64 + 2 * c), last)
            last = jnp.where(lane8 == 2 * c + 1, turn(lower_planes, 65 + 2 * c), last)
        ref[3] = last

    def unpack(ref, c):
        main, last = ref[c], ref[3]
        pick = lambda value, k: jnp.where(lane8 == 64, turn(last, 64 - 2 * c - k), value)
        return jnp.concatenate([pick(main, 0), pick(turn(main, 64), 1)], axis=0)

    def send_faces():
        lefts, rights = [], []
        for c in range(3):
            for k in range(2):
                n = 24 + 2 * c + k
                ve[2 * c + k] = ve[2 * c + k] + q[n // count, n % count]
            value = turn(ve[2 * c], 64)
            for j in range(8):
                value = jnp.where(lane // EY == j, turn(row(c, 0, j), EY * j), value)
            lefts.append(value)
            rights.append(ve[2 * c + 1])
        pack(to_left, lefts)
        pack(to_right, rights)
        for copy in faces:
            copy.start()

    def expand(c, parts):
        def put(n, value):
            out[c, n] = jnp.take_along_axis(value, inverse, axis=1)

        came = unpack(from_left, c)
        edge = ve[2 * c] + jnp.where(lane == 0, turn(came, 64), 0.0)
        if 0 in parts:
            face = ve[2 * c + 1] + unpack(from_right, c)
        for i in parts:
            for j in range(8):
                value = row(c, i, j)
                if i == 0:
                    value = value + jnp.where(lane < EY, turn(came, -EY * j), 0.0)
                    right = jnp.where(below, turn(value, -EY), turn(face, LANES - EY - EY * j))
                    put(72 + j, right)
                if j == 0:
                    top = jnp.where(lower, turn(value, -1), turn(edge, 7 - i))
                    put(9 * i + 8, top)
                    if i == 0:
                        corner = jnp.where(below, turn(top, -EY), turn(face, 63))
                        put(80, jnp.where(lower, turn(right, -1), corner))
                put(9 * i + j, value)

    transform(0)
    come(0)
    go(3)
    go(4)
    transform(1)
    transform(2)
    arrived(recv2, q, 0)
    send_faces()
    come(1)
    come(2)
    for e in range(6):
        @pl.when(me == home[e])
        def _():
            xe[me] = we[e]
            drain(recv_e.at[6], xe.at[rest])
            backe[...] = apply(xe[...].reshape(length, LANES)).reshape(count, depth, LANES)
            qe[e] = backe[me]
            peers(lambda s: remote(backe.at[s], qe.at[e], send_e.at[6], recv_e.at[e], s, dom).start())

    for n in (3, 4):
        transform(n)
        come(n)

    pieces = [(0, 0, 81), (1, 0, 81), (2, 0, 27), (2, 63, 81), (2, 27, 63)]
    stores = [
        pltpu.make_async_copy(out.at[c, a:b], out_hbm.at[c, a:b], store.at[n]) for n, (c, a, b) in enumerate(pieces)
    ]
    arrived(recv2, q, 1)
    arrived(recv2, q, 2)
    for copy in faces:
        copy.wait()
    expand(0, range(8))
    stores[0].start()
    for e in range(6):
        pl.when(me != home[e])(lambda: drain(recv_e.at[e], qe.at[0]))
    arrived(recv2, q, 3)
    expand(1, range(8))
    stores[1].start()
    expand(2, (0, 1, 2, 7))
    stores[2].start()
    stores[3].start()
    arrived(recv2, q, 4)
    expand(2, (3, 4, 5, 6))
    stores[4].start()

    for n in range(5):
        arrived(send1, x, n)
        arrived(send2, x, n)
    for e in range(6):
        pl.when(me != home[e])(lambda: drain(send_e.at[e], we.at[0]))
        pl.when(me == home[e])(lambda: drain(send_e.at[6], xe.at[rest]))
    for copy in stores:
        copy.wait()


def step(slots, geometry, mats, chi, clo, velocity):
    count, doms = lax.axis_size("modes"), lax.axis_size("dom")
    depth = velocity.shape[1] // NODES
    wire = (6 * 32 // count, count, depth, LANES)
    ends = (6, depth, LANES)
    single = (count, depth, LANES)
    face = (4, depth // 2, LANES)
    vmem, dma = pltpu.VMEM, pltpu.SemaphoreType.DMA
    there = pl.BlockSpec(memory_space=pl.ANY)
    return pl.pallas_call(
        functools.partial(kernel, count, doms, depth),
        in_specs=[there] * 6,
        out_specs=there,
        out_shape=jax.ShapeDtypeStruct((3, NODES, depth, LANES), F32),
        scratch_shapes=[
            vmem(slots.shape, jnp.int32),
            vmem(geometry.shape, F32),
            vmem(mats.shape, F32),
            vmem((3, NODES * depth, LANES), F32),
            vmem(chi.shape, BF16),
            vmem(clo.shape, BF16),
            vmem((TALL, LANES), F32),
            vmem((4 * TALL, 2 * LANES), BF16),
            vmem((3 * depth // 2, 256, 2 * LANES), BF16),
            vmem((TALL * depth, LANES), F32),
            vmem(wire, F32),
            vmem(ends, F32),
            vmem((3, ROWS, depth, LANES), F32),
            vmem(ends, F32),
            vmem(wire, F32),
            vmem(single, F32),
            vmem(wire, F32),
            vmem(single, F32),
            vmem(wire, F32),
            vmem(ends, F32),
            vmem(face, F32),
            vmem(face, F32),
            vmem(face, F32),
            vmem(face, F32),
            vmem((3, NODES, depth, LANES), F32),
            dma((8,)),
            dma((5,)),
            dma((5,)),
            dma((5,)),
            dma((5,)),
            dma((7,)),
            dma((7,)),
            dma((2,)),
            dma((2,)),
            dma((5,)),
        ],
        compiler_params=pltpu.CompilerParams(collective_id=0, has_side_effects=True),
        name="step",
    )(slots, geometry, mats, chi, clo, velocity)


def body(velocity, slot_of_cell, elem_mats, geometry):
    depth = velocity.shape[1]
    table = coupling(depth * lax.axis_size("modes"))
    chi = np.asarray(table, np.float32).astype(jnp.bfloat16)
    clo = (table - chi.astype(np.float64)).astype(np.float32).astype(jnp.bfloat16)
    flat = jnp.swapaxes(velocity, 1, 2).reshape(3, NODES * depth, LANES)
    result = step(slot_of_cell, geometry, jnp.swapaxes(elem_mats, 0, 1), jnp.asarray(chi), jnp.asarray(clo), flat)
    return jnp.swapaxes(result, 1, 2)


def solution(mesh):
    in_specs = (P(None, "modes", None, "dom"), P("dom", None), P(), P(None, "dom"))
    out_specs = P(None, "modes", None, "dom")
    return jax.shard_map(body, mesh=mesh, in_specs=in_specs, out_specs=out_specs, check_vma=False)
```

time: 98.3 us -> 90.6 us (0.922)
  Pallas kernels: 93.4 us -> 87.5 us
  local copies, waits for them, and re-layouts: 4.6 us -> 3 us
    pallas_call x1, Pallas kernels: 93.4 us -> 87.5 us  [step(): pl.pallas_call(functools.partial(kernel, count, doms, depth), in_specs=[t...]
    unnamed x2 -> x1, local copies, waits for them, and re-layouts: 4.6 us -> 3 us
where the time goes in v1:
time: 90.6 us; the launch traced here: 90.5 us
  Pallas kernels  87.5 us (97%)
  local copies, waits for them, and re-layouts  3 us (3%)
    pallas_call x1, Pallas kernels, step(): pl.pallas_call(functools.partial(kernel, count, doms, depth), in_specs=[t...  87.5 us
    unnamed x1, local copies, waits for them, and re-layouts  3 us

profile of v1, /device:TPU:1, one launch (start us, length us, event | category | flops | bytes accessed | tf_op | source)
XLA Modules:
  0.0 90.5 jit_solution(13224319535511825042)
XLA Ops:
  0.0 87.5 %step.1 = f32[3,81,16,128]{3,2,1,0:T(8,128)} custom-call(s32[1,128]{1,0:T(1,128)} %slot_hbm.1, f32[4,128]{1,0:T(4,128)} %geo_hbm.1, f32[81,4,81]{2,1,0:T(4,128)} %bitcast.7, bf16[512,512]{1,0:T(8,128)(2,1)} %constant.4.clone.chi_hbm, bf16[512,512]{1,0:T(8,128)(2,1)} %constant.5.clone.clo_hbm, f32[3,1296,128]{2,1,0:T(8,128)} %bitcast.6), custom_call_target="tpu_custom_call" | custom-call | tf_op jit(solution)/shard_map/step/pallas_call | solution.py:401
  87.5 3.0 %copy.8 = f32[3,16,81,128]{3,1,2,0:T(8,128)} copy(f32[3,16,81,128]{3,1,2,0:T(8,128)} %bitcast.5) | data formatting | bytes 3981312

commit v2 on v1

--- a/solution.py
+++ b/solution.py
@@ -54,10 +54,10 @@
 
 def kernel(
     count, doms, depth,
-    slot_hbm, geo_hbm, mats_hbm, chi_hbm, clo_hbm, vel_hbm, out_hbm,
+    slot_hbm, geo_hbm, mats_hbm, chi_hbm, clo_hbm, vel_hbm, out,
     slot_ref, geo_ref, mats_ref, vel, chi, clo, stage, lhs, rhs, tall,
-    w, we, v, ve, x, xe, back, backe, q, qe, to_left, to_right, from_left, from_right, out,
-    load, send1, recv1, send2, recv2, send_e, recv_e, send_f, recv_f, store,
+    w, we, v, ve, x, xe, back, backe, q, qe, to_left, to_right, from_left, from_right,
+    load, send1, recv1, send2, recv2, send_e, recv_e, send_f, recv_f, hello,
 ):
     unit = 32 // count
     chunks = [(0, 1), (1, 2), (2, 3), (3, 5), (5, 6)]
@@ -94,8 +94,13 @@
     small = ((slot_hbm, slot_ref), (geo_hbm, geo_ref), (mats_hbm, mats_ref))
     loads += [pltpu.make_async_copy(src, dst, load.at[5 + n]) for n, (src, dst) in enumerate(small)]
     barrier = pltpu.get_barrier_semaphore()
-    for other in (before, after):
-        pl.semaphore_signal(barrier, inc=1, device_id=(me, other), device_id_type=MESH)
+    gate = max(count // 2 - 4, 0)
+
+    @pl.when(me == gate)
+    def _():
+        for other in (before, after):
+            pl.semaphore_signal(barrier, inc=1, device_id=(me, other), device_id_type=MESH)
+
     peers(lambda d: pl.semaphore_signal(barrier, inc=1, device_id=(d, dom), device_id_type=MESH))
     for n in (7, 5, 6, 0, 1, 2, 3, 4):
         loads[n].start()
@@ -229,7 +234,8 @@
     loads[0].wait()
     loads[1].wait()
     mass(0)
-    pl.semaphore_wait(barrier, count + 1)
+    pl.when(me != gate)(lambda: pl.semaphore_wait(barrier, count - 1))
+    pl.when(me == gate)(lambda: pl.semaphore_wait(barrier, count + 1))
     go(1)
     loads[2].wait()
     mass(1)
@@ -334,13 +340,26 @@
                         put(80, jnp.where(lower, turn(right, -1), corner))
                 put(9 * i + j, value)
 
+    @pl.when(me == gate)
+    def _():
+        for n, other in enumerate((before, after)):
+            pl.semaphore_signal(hello.at[n], inc=1, device_id=(me, other), device_id_type=MESH)
+
     transform(0)
     come(0)
     go(3)
     go(4)
+
+    @pl.when(me == gate)
+    def _():
+        for n in range(2):
+            pl.semaphore_wait(hello.at[n], 1)
+        peers(lambda d: pl.semaphore_signal(hello.at[2], inc=1, device_id=(d, dom), device_id_type=MESH))
+
     transform(1)
     transform(2)
     arrived(recv2, q, 0)
+    pl.when(me != gate)(lambda: pl.semaphore_wait(hello.at[2], 1))
     send_faces()
     come(1)
     come(2)
@@ -357,27 +376,18 @@
         transform(n)
         come(n)
 
-    pieces = [(0, 0, 81), (1, 0, 81), (2, 0, 27), (2, 63, 81), (2, 27, 63)]
-    stores = [
-        pltpu.make_async_copy(out.at[c, a:b], out_hbm.at[c, a:b], store.at[n]) for n, (c, a, b) in enumerate(pieces)
-    ]
     arrived(recv2, q, 1)
     arrived(recv2, q, 2)
     for copy in faces:
         copy.wait()
     expand(0, range(8))
-    stores[0].start()
     for e in range(6):
         pl.when(me != home[e])(lambda: drain(recv_e.at[e], qe.at[0]))
     arrived(recv2, q, 3)
     expand(1, range(8))
-    stores[1].start()
     expand(2, (0, 1, 2, 7))
-    stores[2].start()
-    stores[3].start()
     arrived(recv2, q, 4)
     expand(2, (3, 4, 5, 6))
-    stores[4].start()
 
     for n in range(5):
         arrived(send1, x, n)
@@ -385,8 +395,6 @@
     for e in range(6):
         pl.when(me != home[e])(lambda: drain(send_e.at[e], we.at[0]))
         pl.when(me == home[e])(lambda: drain(send_e.at[6], xe.at[rest]))
-    for copy in stores:
-        copy.wait()
 
 
 def step(slots, geometry, mats, chi, clo, velocity):
@@ -401,8 +409,8 @@
     return pl.pallas_call(
         functools.partial(kernel, count, doms, depth),
         in_specs=[there] * 6,
-        out_specs=there,
-        out_shape=jax.ShapeDtypeStruct((3, NODES, depth, LANES), F32),
+        out_specs=pl.BlockSpec(memory_space=pltpu.VMEM),
+        out_shape=pltpu.VMEM((3, NODES, depth, LANES), F32),
         scratch_shapes=[
             vmem(slots.shape, jnp.int32),
             vmem(geometry.shape, F32),
@@ -428,7 +436,6 @@
             vmem(face, F32),
             vmem(face, F32),
             vmem(face, F32),
-            vmem((3, NODES, depth, LANES), F32),
             dma((8,)),
             dma((5,)),
             dma((5,)),
@@ -438,7 +445,7 @@
             dma((7,)),
             dma((2,)),
             dma((2,)),
-            dma((5,)),
+            pltpu.SemaphoreType.REGULAR((3,)),
         ],
         compiler_params=pltpu.CompilerParams(collective_id=0, has_side_effects=True),
         name="step",

time: 90.6 us -> 85.1 us (0.939)
  Pallas kernels: 87.5 us -> 83.7 us
  local copies, waits for them, and re-layouts: 3 us -> 1.28 us
    pallas_call x1, Pallas kernels: 87.5 us -> 83.7 us  [step(): pl.pallas_call(functools.partial(kernel, count, doms, depth), in_specs=[t...]
    unnamed x1, local copies, waits for them, and re-layouts: 3 us -> 1.28 us
where the time goes in v2:
time: 85.1 us; the launch traced here: 85 us
  Pallas kernels  83.7 us (98%)
  local copies, waits for them, and re-layouts  1.28 us (2%)
    pallas_call x1, Pallas kernels, step(): pl.pallas_call(functools.partial(kernel, count, doms, depth), in_specs=[t...  83.7 us

profile of v2, /device:TPU:1, one launch (start us, length us, event | category | flops | bytes accessed | tf_op | source)
XLA Modules:
  0.0 85.0 jit_solution(17968149781242950494)
XLA Ops:
  0.0 83.7 %step.1 = f32[3,81,16,128]{3,2,1,0:T(8,128)S(1)} custom-call(s32[1,128]{1,0:T(1,128)} %slot_hbm.1, f32[4,128]{1,0:T(4,128)} %geo_hbm.1, f32[81,4,81]{2,1,0:T(4,128)} %bitcast.7, bf16[512,512]{1,0:T(8,128)(2,1)} %constant.4.clone.chi_hbm, bf16[512,512]{1,0:T(8,128)(2,1)} %constant.5.clone.clo_hbm, f32[3,1296,128]{2,1,0:T(8,128)} %bitcast.6), custom_call_target="tpu_custom_call" | custom-call | tf_op jit(solution)/shard_map/step/pallas_call | solution.py:409
  83.7 1.3 %copy.8 = f32[3,16,81,128]{3,1,2,0:T(8,128)} copy(f32[3,16,81,128]{3,1,2,0:T(8,128)S(1)} %bitcast.5) | data formatting | bytes 3981312

commit v3 on v2

--- a/solution.py
+++ b/solution.py
@@ -56,8 +56,8 @@
     count, doms, depth,
     slot_hbm, geo_hbm, mats_hbm, chi_hbm, clo_hbm, vel_hbm, out,
     slot_ref, geo_ref, mats_ref, vel, chi, clo, stage, lhs, rhs, tall,
-    w, we, v, ve, x, xe, back, backe, q, qe, to_left, to_right, from_left, from_right,
-    load, send1, recv1, send2, recv2, send_e, recv_e, send_f, recv_f, hello,
+    w, we, v, ve, line, x, xe, back, backe, q, qe, to_left, to_right, from_left, from_right,
+    load, send_z, recv_z, send1, recv1, send2, recv2, send_e, recv_e, send_f, recv_f, hello,
 ):
     unit = 32 // count
     chunks = [(0, 1), (1, 2), (2, 3), (3, 5), (5, 6)]
@@ -95,13 +95,27 @@
     loads += [pltpu.make_async_copy(src, dst, load.at[5 + n]) for n, (src, dst) in enumerate(small)]
     barrier = pltpu.get_barrier_semaphore()
     gate = max(count // 2 - 4, 0)
+    planes = count // 8
+    zme, yme = me // 8, lax.rem(me, 8)
+    line_peers = [lax.rem(zme + high, planes) * 8 + yme for high in range(1, planes)]
+    plane_peers = [zme * 8 + lax.rem(yme + low, 8) for low in range(1, 8)]
+    heard = planes - 1 + 7
+
+    def signal(sem, modes, where):
+        pl.semaphore_signal(sem, inc=1, device_id=(modes, where), device_id_type=MESH)
+
+    for d in line_peers + plane_peers:
+        signal(barrier, d, dom)
+
+    @pl.when((yme == gate % 8) & (zme != gate // 8))
+    def _():
+        signal(barrier, gate + 1, dom)
 
     @pl.when(me == gate)
     def _():
         for other in (before, after):
-            pl.semaphore_signal(barrier, inc=1, device_id=(me, other), device_id_type=MESH)
-
-    peers(lambda d: pl.semaphore_signal(barrier, inc=1, device_id=(d, dom), device_id_type=MESH))
+            signal(barrier, me, other)
+
     for n in (7, 5, 6, 0, 1, 2, 3, 4):
         loads[n].start()
     for n in (5, 6, 7):
@@ -220,7 +234,7 @@
 
     def go(n):
         a, size = spans[n]
-        peers(lambda d: remote(w.at[pl.ds(a, size), d], x.at[pl.ds(a, size), me], send1.at[n], recv1.at[n], d, dom).start())
+        peers(lambda d: remote(w.at[pl.ds(a, size), d], x.at[pl.ds(a, size), zme, yme], send1.at[n], recv1.at[n], d, dom).start())
 
     def come(n):
         a, size = spans[n]
@@ -234,12 +248,38 @@
     loads[0].wait()
     loads[1].wait()
     mass(0)
-    pl.when(me != gate)(lambda: pl.semaphore_wait(barrier, count - 1))
-    pl.when(me == gate)(lambda: pl.semaphore_wait(barrier, count + 1))
-    go(1)
+    pl.when((me != gate) & (me != gate + 1))(lambda: pl.semaphore_wait(barrier, heard))
+    pl.when(me == gate)(lambda: pl.semaphore_wait(barrier, heard + 2))
+    pl.when(me == gate + 1)(lambda: pl.semaphore_wait(barrier, heard + planes - 1))
+
+    @pl.when(me != gate)
+    def _():
+        for d in plane_peers:
+            signal(hello.at[3], d, dom)
+
+    own = pl.ds(unit, unit)
+    for d in line_peers:
+        block = w.at[own, pl.ds(d - yme, 8)]
+        remote(block, line.at[:, zme], send_z.at[0], recv_z.at[0], d, dom).start()
+    for k in range(unit):
+        for n in range(8):
+            line[k, zme, n] = w[unit + k, zme * 8 + n]
+
+    def relay():
+        if planes > 1:
+            drain(recv_z.at[0], line.at[:, pl.ds(0, planes - 1)])
+        for d in plane_peers:
+            src, dst = line.at[:, :, d - zme * 8], x.at[own, :, yme]
+            remote(src, dst, send1.at[1], recv1.at[1], d, dom).start()
+        for k in range(unit):
+            for z in range(planes):
+                x[unit + k, z, yme] = line[k, z, yme]
+
     loads[2].wait()
     mass(1)
     mass(2)
+    pl.when((me == gate) | (zme != gate // 8))(lambda: pl.semaphore_wait(hello.at[3], 7))
+    pl.when((me != gate) & (zme == gate // 8))(lambda: pl.semaphore_wait(hello.at[3], 6))
     go(0)
     for e in range(6):
         @pl.when(me != home[e])
@@ -248,8 +288,10 @@
     go(2)
     for t in range(3):
         stack(t)
-    for c in range(3):
-        stiff(c)
+    stiff(0)
+    relay()
+    stiff(1)
+    stiff(2)
     loads[3].wait()
     loads[4].wait()
 
@@ -260,9 +302,12 @@
 
     def transform(n):
         a, size = spans[n]
-        arrived(recv1, x, n)
-        for r in range(a, a + size):
-            x[r, me] = w[r, me]
+        if n == 1:
+            drain(recv1.at[1], w.at[own, pl.ds(0, 7 * planes)])
+        else:
+            arrived(recv1, w, n)
+            for r in range(a, a + size):
+                x[r, zme, yme] = w[r, me]
         for r in range(a, a + size, 2):
             two = range(r, min(r + 2, a + size))
             value = apply(jnp.concatenate([x[k].reshape(length, LANES) for k in two], axis=1))
@@ -343,7 +388,7 @@
     @pl.when(me == gate)
     def _():
         for n, other in enumerate((before, after)):
-            pl.semaphore_signal(hello.at[n], inc=1, device_id=(me, other), device_id_type=MESH)
+            signal(hello.at[n], me, other)
 
     transform(0)
     come(0)
@@ -354,7 +399,7 @@
     def _():
         for n in range(2):
             pl.semaphore_wait(hello.at[n], 1)
-        peers(lambda d: pl.semaphore_signal(hello.at[2], inc=1, device_id=(d, dom), device_id_type=MESH))
+        peers(lambda d: signal(hello.at[2], d, dom))
 
     transform(1)
     transform(2)
@@ -390,8 +435,13 @@
     expand(2, (3, 4, 5, 6))
 
     for n in range(5):
-        arrived(send1, x, n)
-        arrived(send2, x, n)
+        if n == 1:
+            drain(send1.at[1], w.at[own, pl.ds(0, 7 * planes)])
+        else:
+            arrived(send1, w, n)
+        arrived(send2, w, n)
+    if planes > 1:
+        drain(send_z.at[0], line.at[:, pl.ds(0, planes - 1)])
     for e in range(6):
         pl.when(me != home[e])(lambda: drain(send_e.at[e], we.at[0]))
         pl.when(me == home[e])(lambda: drain(send_e.at[6], xe.at[rest]))
@@ -426,7 +476,8 @@
             vmem(ends, F32),
             vmem((3, ROWS, depth, LANES), F32),
             vmem(ends, F32),
-            vmem(wire, F32),
+            vmem((wire[0] // 6, count // 8, 8) + wire[2:], F32),
+            vmem((wire[0], count // 8, 8) + wire[2:], F32),
             vmem(single, F32),
             vmem(wire, F32),
             vmem(single, F32),
@@ -437,6 +488,8 @@
             vmem(face, F32),
             vmem(face, F32),
             dma((8,)),
+            dma((1,)),
+            dma((1,)),
             dma((5,)),
             dma((5,)),
             dma((5,)),
@@ -445,7 +498,7 @@
             dma((7,)),
             dma((2,)),
             dma((2,)),
-            pltpu.SemaphoreType.REGULAR((3,)),
+            pltpu.SemaphoreType.REGULAR((4,)),
         ],
         compiler_params=pltpu.CompilerParams(collective_id=0, has_side_effects=True),
         name="step",

time: 85.1 us -> 83.9 us (0.986)
  Pallas kernels: 83.7 us -> 82.5 us
    pallas_call x1, Pallas kernels: 83.7 us -> 82.5 us  [step(): pl.pallas_call(functools.partial(kernel, count, doms, depth), in_specs=[t...]
where the time goes in v3:
time: 83.9 us; the launch traced here: 83.8 us
  Pallas kernels  82.5 us (98%)
  local copies, waits for them, and re-layouts  1.28 us (2%)
    pallas_call x1, Pallas kernels, step(): pl.pallas_call(functools.partial(kernel, count, doms, depth), in_specs=[t...  82.5 us

profile of v3, /device:TPU:1, one launch (start us, length us, event | category | flops | bytes accessed | tf_op | source)
XLA Modules:
  0.0 83.8 jit_solution(9319799488553509305)
XLA Ops:
  0.0 82.5 %step.1 = f32[3,81,16,128]{3,2,1,0:T(8,128)S(1)} custom-call(s32[1,128]{1,0:T(1,128)} %slot_hbm.1, f32[4,128]{1,0:T(4,128)} %geo_hbm.1, f32[81,4,81]{2,1,0:T(4,128)} %bitcast.7, bf16[512,512]{1,0:T(8,128)(2,1)} %constant.4.clone.chi_hbm, bf16[512,512]{1,0:T(8,128)(2,1)} %constant.5.clone.clo_hbm, f32[3,1296,128]{2,1,0:T(8,128)} %bitcast.6), custom_call_target="tpu_custom_call" | custom-call | tf_op jit(solution)/shard_map/step/pallas_call | solution.py:459
  82.5 1.3 %copy.8 = f32[3,16,81,128]{3,1,2,0:T(8,128)} copy(f32[3,16,81,128]{3,1,2,0:T(8,128)S(1)} %bitcast.5) | data formatting | bytes 3981312

commit v4 on v3

--- a/solution.py
+++ b/solution.py
@@ -57,6 +57,7 @@
     slot_hbm, geo_hbm, mats_hbm, chi_hbm, clo_hbm, vel_hbm, out,
     slot_ref, geo_ref, mats_ref, vel, chi, clo, stage, lhs, rhs, tall,
     w, we, v, ve, line, x, xe, back, backe, q, qe, to_left, to_right, from_left, from_right,
+    end_left, end_right, end_from_left, end_from_right,
     load, send_z, recv_z, send1, recv1, send2, recv2, send_e, recv_e, send_f, recv_f, hello,
 ):
     unit = 32 // count
@@ -66,7 +67,6 @@
     me, dom = lax.axis_index("modes"), lax.axis_index("dom")
     after, before = lax.rem(dom + 1, doms), lax.rem(dom + doms - 1, doms)
     home = homes(count)
-    far = [2, 1, 3, 0] if count == 32 else list(range(count // 8))
 
     def remote(src, dst, send, recv, modes, where):
         return pltpu.make_async_remote_copy(
@@ -76,18 +76,18 @@
     def drain(sem, ref):
         pltpu.make_async_copy(ref, ref, sem).wait()
 
+    planes = count // 8
+
+    order = [2, 1, 3, 0] if planes == 4 else range(planes)
+
     def peers(act):
-        def some(low, _):
-            for high in far:
-                z = lax.rem(me // 8 + high, len(far))
-                d = z * 8 + lax.rem(lax.rem(me, 8) + low, 8)
-                if high:
-                    act(d)
-                else:
-                    pl.when(low > 0)(lambda: act(d))
-            return 0
-
-        lax.fori_loop(0, 8, some, 0)
+        for high in order:
+            def some(n, _):
+                z = lax.rem(me // 8 + high, planes)
+                act(z * 8 + lax.rem(lax.rem(me, 8) + n, 8))
+                return 0
+
+            lax.fori_loop(2 if high else 1, 10 if high else 8, some, 0)
 
     loads = [pltpu.make_async_copy(vel_hbm.at[c], vel.at[c], load.at[c]) for c in range(3)]
     loads += [pltpu.make_async_copy(chi_hbm, chi, load.at[3]), pltpu.make_async_copy(clo_hbm, clo, load.at[4])]
@@ -95,7 +95,6 @@
     loads += [pltpu.make_async_copy(src, dst, load.at[5 + n]) for n, (src, dst) in enumerate(small)]
     barrier = pltpu.get_barrier_semaphore()
     gate = max(count // 2 - 4, 0)
-    planes = count // 8
     zme, yme = me // 8, lax.rem(me, 8)
     line_peers = [lax.rem(zme + high, planes) * 8 + yme for high in range(1, planes)]
     plane_peers = [zme * 8 + lax.rem(yme + low, 8) for low in range(1, 8)]
@@ -330,21 +329,23 @@
     faces = [
         remote(to_left, from_right, send_f.at[0], recv_f.at[0], me, before),
         remote(to_right, from_left, send_f.at[1], recv_f.at[1], me, after),
+        remote(end_left, end_from_right, send_f.at[2], recv_f.at[2], me, before),
+        remote(end_right, end_from_left, send_f.at[3], recv_f.at[3], me, after),
     ]
 
-    def pack(ref, values):
-        last = jnp.zeros((8, LANES), F32)
+    plane = lax.broadcasted_iota(jnp.int32, (depth, LANES), 0)
+
+    def pack(ref, end, values):
+        last = jnp.zeros((depth, LANES), F32)
         for c, value in enumerate(values):
-            upper_planes, lower_planes = value[0:8], value[8:16]
-            ref[c] = jnp.where(lane8 < 64, upper_planes, turn(lower_planes, 64))
-            last = jnp.where(lane8 == 2 * c, turn(upper_planes, 64 + 2 * c), last)
-            last = jnp.where(lane8 == 2 * c + 1, turn(lower_planes, 65 + 2 * c), last)
-        ref[3] = last
-
-    def unpack(ref, c):
-        main, last = ref[c], ref[3]
-        pick = lambda value, k: jnp.where(lane8 == 64, turn(last, 64 - 2 * c - k), value)
-        return jnp.concatenate([pick(main, 0), pick(turn(main, 64), 1)], axis=0)
+            ref[c] = jnp.where(lane8 < 64, value[0:8], turn(value[8:16], 64))
+            last = jnp.where(lane == depth * c + plane, jnp.broadcast_to(value[:, 64:65], (depth, LANES)), last)
+        end[...] = jnp.sum(last, axis=0, keepdims=True)
+
+    def unpack(ref, end, c):
+        last = jnp.where(lane == depth * c + plane, jnp.broadcast_to(end[...], (depth, LANES)), 0.0)
+        value = jnp.concatenate([ref[c], turn(ref[c], 64)], axis=0)
+        return jnp.where(lane == 64, jnp.sum(last, axis=1, keepdims=True), value)
 
     def send_faces():
         lefts, rights = [], []
@@ -357,8 +358,8 @@
                 value = jnp.where(lane // EY == j, turn(row(c, 0, j), EY * j), value)
             lefts.append(value)
             rights.append(ve[2 * c + 1])
-        pack(to_left, lefts)
-        pack(to_right, rights)
+        pack(to_left, end_left, lefts)
+        pack(to_right, end_right, rights)
         for copy in faces:
             copy.start()
 
@@ -366,10 +367,10 @@
         def put(n, value):
             out[c, n] = jnp.take_along_axis(value, inverse, axis=1)
 
-        came = unpack(from_left, c)
+        came = unpack(from_left, end_from_left, c)
         edge = ve[2 * c] + jnp.where(lane == 0, turn(came, 64), 0.0)
         if 0 in parts:
-            face = ve[2 * c + 1] + unpack(from_right, c)
+            face = ve[2 * c + 1] + unpack(from_right, end_from_right, c)
         for i in parts:
             for j in range(8):
                 value = row(c, i, j)
@@ -453,7 +454,7 @@
     wire = (6 * 32 // count, count, depth, LANES)
     ends = (6, depth, LANES)
     single = (count, depth, LANES)
-    face = (4, depth // 2, LANES)
+    face, end = (3, depth // 2, LANES), (1, LANES)
     vmem, dma = pltpu.VMEM, pltpu.SemaphoreType.DMA
     there = pl.BlockSpec(memory_space=pl.ANY)
     return pl.pallas_call(
@@ -487,6 +488,10 @@
             vmem(face, F32),
             vmem(face, F32),
             vmem(face, F32),
+            vmem(end, F32),
+            vmem(end, F32),
+            vmem(end, F32),
+            vmem(end, F32),
             dma((8,)),
             dma((1,)),
             dma((1,)),
@@ -496,8 +501,8 @@
             dma((5,)),
             dma((7,)),
             dma((7,)),
-            dma((2,)),
-            dma((2,)),
+            dma((4,)),
+            dma((4,)),
             pltpu.SemaphoreType.REGULAR((4,)),
         ],
         compiler_params=pltpu.CompilerParams(collective_id=0, has_side_effects=True),

time: 83.9 us -> 82.6 us (0.985)
  Pallas kernels: 82.5 us -> 81.2 us
    pallas_call x1, Pallas kernels: 82.5 us -> 81.2 us  [step(): pl.pallas_call(functools.partial(kernel, count, doms, depth), in_specs=[t...]
where the time goes in v4:
time: 82.6 us; the launch traced here: 82.5 us
  Pallas kernels  81.2 us (98%)
  local copies, waits for them, and re-layouts  1.28 us (2%)
    pallas_call x1, Pallas kernels, step(): pl.pallas_call(functools.partial(kernel, count, doms, depth), in_specs=[t...  81.2 us

profile of v4, /device:TPU:1, one launch (start us, length us, event | category | flops | bytes accessed | tf_op | source)
XLA Modules:
  0.0 82.5 jit_solution(10077151280146197804)
XLA Ops:
  0.0 81.2 %step.1 = f32[3,81,16,128]{3,2,1,0:T(8,128)S(1)} custom-call(s32[1,128]{1,0:T(1,128)} %slot_hbm.1, f32[4,128]{1,0:T(4,128)} %geo_hbm.1, f32[81,4,81]{2,1,0:T(4,128)} %bitcast.7, bf16[512,512]{1,0:T(8,128)(2,1)} %constant.4.clone.chi_hbm, bf16[512,512]{1,0:T(8,128)(2,1)} %constant.5.clone.clo_hbm, f32[3,1296,128]{2,1,0:T(8,128)} %bitcast.6), custom_call_target="tpu_custom_call" | custom-call | tf_op jit(solution)/shard_map/step/pallas_call | solution.py:460
  81.2 1.3 %copy.8 = f32[3,16,81,128]{3,1,2,0:T(8,128)} copy(f32[3,16,81,128]{3,1,2,0:T(8,128)S(1)} %bitcast.5) | data formatting | bytes 3981312

commit v5 on v4

--- a/solution.py
+++ b/solution.py
@@ -39,7 +39,7 @@
 
 
 def homes(count):
-    return [8, 19, 13, 22, 3, 28] if count == 32 else list(range(6))
+    return [0, 27, 5, 30, 2, 29] if count == 32 else list(range(6))
 
 
 def place(c, i, j):
@@ -78,7 +78,7 @@
 
     planes = count // 8
 
-    order = [2, 1, 3, 0] if planes == 4 else range(planes)
+    order = [2, 3, 1, 0] if planes == 4 else range(planes)
 
     def peers(act):
         for high in order:
@@ -195,7 +195,7 @@
                 tall[pl.ds(2 * step + h, TALL, stride=depth), :] = image[:, LANES * h : LANES * h + LANES] * scale
             return 0
 
-        lax.fori_loop(0, depth // 2, pair, 0, unroll=2)
+        lax.fori_loop(0, depth // 2, pair, 0, unroll=4)
 
         def rows(i, j, value):
             n = place(c, i, j)
@@ -221,7 +221,7 @@
                 tall[pl.ds(2 * step + h, TALL, stride=depth), :] = (terms[0] + terms[1]) + (terms[2] + terms[3])
             return 0
 
-        lax.fori_loop(0, depth // 2, pair, 0, unroll=2)
+        lax.fori_loop(0, depth // 2, pair, 0, unroll=4)
 
         def rows(i, j, value):
             v[c, 8 * i + j] = value

time: 82.6 us -> 82 us (level)
  no operation moved by 1% of the time
where the time goes in v5:
time: 82 us; the launch traced here: 81.9 us
  Pallas kernels  80.6 us (98%)
  local copies, waits for them, and re-layouts  1.28 us (2%)
    pallas_call x1, Pallas kernels, step(): pl.pallas_call(functools.partial(kernel, count, doms, depth), in_specs=[t...  80.6 us

profile of v5, /device:TPU:1, one launch (start us, length us, event | category | flops | bytes accessed | tf_op | source)
XLA Modules:
  0.0 81.9 jit_solution(468840303972070121)
XLA Ops:
  0.0 80.6 %step.1 = f32[3,81,16,128]{3,2,1,0:T(8,128)S(1)} custom-call(s32[1,128]{1,0:T(1,128)} %slot_hbm.1, f32[4,128]{1,0:T(4,128)} %geo_hbm.1, f32[81,4,81]{2,1,0:T(4,128)} %bitcast.7, bf16[512,512]{1,0:T(8,128)(2,1)} %constant.4.clone.chi_hbm, bf16[512,512]{1,0:T(8,128)(2,1)} %constant.5.clone.clo_hbm, f32[3,1296,128]{2,1,0:T(8,128)} %bitcast.6), custom_call_target="tpu_custom_call" | custom-call | tf_op jit(solution)/shard_map/step/pallas_call | solution.py:460
  80.7 1.3 %copy.8 = f32[3,16,81,128]{3,1,2,0:T(8,128)} copy(f32[3,16,81,128]{3,1,2,0:T(8,128)S(1)} %bitcast.5) | data formatting | bytes 3981312
